TPU v7x, 32 devices: a whole 2x2x4 slice. The times are simulated.
32 devices in a mesh: rows: 8 (over z, y), code: 4 (over x, core).
Axes of the slice: x: 2, y: 2, z: 4, core: 2. Of those that a mesh axis runs over, the one named last changes fastest.
Arguments:
- embedding_vectors: bfloat16 [3072, 256], P('rows'), may hold values from -45.3125 to 45.3125
- codebook: bfloat16 [65536, 256], P(('code', 'rows')), may hold values from -0.38125 to 0.38125
- weights: float32 [3072], P('rows'), may hold values from 0.6 to 4.2
Outputs:
- gradient: float32 [65536, 256], P(('code', 'rows'))
- load: float32 [65536], P(('code', 'rows'))
All inputs are finite; a program needn't handle non-finite values.
Results may differ from a plain program's by a relative error of at most 0.013.
Values may be sent and summed in bfloat16 or wider, within the bound.
No kernel may reach another device: no remote copies, remote signals or barrier semaphores. Data moves between devices by JAX's collectives and lax.ppermute only.
A program may use at most 128 MiB of HBM per device.

v0:
```python
import jax
import jax.numpy as jnp
from jax import lax
from jax.sharding import PartitionSpec as P

ITERS = 3
sharpness_factor = 2.0


def local(embedding_vectors, codebook, weights):
    code_devices = lax.axis_size("code")
    balance = embedding_vectors.shape[0] / (code_devices * codebook.shape[0])
    similarity_table = sharpness_factor * jnp.einsum(
        "nd,kd->nk",
        embedding_vectors,
        lax.all_gather(codebook, "rows", axis=0, tiled=True),
        preferred_element_type=jnp.float32,
    )
    row_peak = lax.pmax(jnp.max(similarity_table, axis=1), "code")
    power_term = jnp.exp(similarity_table - row_peak[:, None])

    def marginal_per_sample(col_scale):
        return lax.psum(jnp.dot(power_term, col_scale, precision=lax.Precision.HIGHEST), "code")

    col_scale = jnp.ones((power_term.shape[1],), jnp.float32)
    row_scale = weights / marginal_per_sample(col_scale)
    for iteration in range(ITERS):
        partial_cols = jnp.dot(row_scale, power_term, precision=lax.Precision.HIGHEST)
        col_scale = balance / lax.psum(partial_cols, "rows")
        row_scale = weights / marginal_per_sample(col_scale)
    transport_plan = power_term * row_scale[:, None] * col_scale[None, :]
    local_mass = jnp.sum(transport_plan, axis=0)
    partial_aggregates = jnp.einsum(
        "nk,nd->kd",
        transport_plan.astype(jnp.bfloat16),
        embedding_vectors,
        preferred_element_type=jnp.float32,
    )
    codeword_sums, code_mass = (
        lax.psum_scatter(partial_aggregates, "rows", scatter_dimension=0, tiled=True),
        lax.psum_scatter(local_mass, "rows", scatter_dimension=0, tiled=True),
    )
    gradient = (code_mass[:, None] * codebook.astype(jnp.float32) - codeword_sums) / balance
    return (gradient, code_mass / balance)


def solution(mesh):
    placed = (P("rows", None), P(("code", "rows"), None), P("rows"))
    return jax.shard_map(
        local,
        mesh=mesh,
        in_specs=placed,
        out_specs=(P(("code", "rows"), None), P(("code", "rows"))),
        check_vma=False,
    )
```

profile of v0, /device:TPU:0, one launch (start us, length us, event | category | flops | bytes accessed | tf_op | source)
XLA Modules:
  0.0 927.6 jit_solution(9325484149887483975)
XLA Ops:
  8.0 129.8 %all-gather.2.cloned.1.call-done = bf16[16384,256]{1,0:T(8,128)(2,1)} async-done(((bf16[2048,256]{1,0:T(8,128)(2,1)}), bf16[16384,256]{1,0:T(8,128)(2,1)}) %all-gather.2.cloned.1.call-update) | async-done | bytes 8388624 | tf_op jit(solution)/shard_map/all_gather | solution.py:16
  137.8 15.2 %fusion.11 = (f32[384]{0:T(512)S(1)}, f32[384,16384]{1,0:T(8,128)}) fusion(bf16[384,256]{1,0:T(8,128)(2,1)S(1)} %copy-done, bf16[16384,256]{1,0:T(8,128)(2,1)} %all-gather.2.cloned.1.call-done), kind=kOutput, calls=%fused_computation.22 | convolution fusion | flops 3233807872 | bytes 33752576 | tf_op jit(solution)/shard_map/nd,kd->nk/dot_general | solution.py:13
  153.0 6.1 pmax.7
  159.1 26.1 %convolution_reduce_fusion.3 = f32[384]{0:T(512)S(1)} fusion(f32[384,16384]{1,0:T(8,128)} %get-tuple-element.5, f32[384]{0:T(512)S(1)} %pmax.7), kind=kOutput, calls=%fused_computation.12 | convolution fusion | flops 81788928 | bytes 25168896 | tf_op jit(solution)/shard_map/dot_general | solution.py:23
  185.2 6.6 psum.49
  191.8 18.6 %fusion.10 = f32[1,16384]{1,0:T(1,128)} fusion(f32[384,1]{0,1:T(1,128)S(1)} %reshape.10, f32[384,16384]{1,0:T(8,128)} %get-tuple-element.5, f32[384]{0:T(512)S(1)} %pmax.7), kind=kOutput, calls=%fused_computation.21 | convolution fusion | flops 81788928 | bytes 25234432 | tf_op jit(solution)/shard_map/dot_general | solution.py:28
  210.6 66.2 %all-reduce.6.cloned.1.call-done = f32[16384]{0:T(1024)} async-done(((f32[16384]{0:T(1024)}), f32[16384]{0:T(1024)}) %all-reduce.6.cloned.1.call-update) | async-done | bytes 65552 | tf_op jit(solution)/shard_map/psum | solution.py:29
  276.8 0.9 broadcast_divide_fusion.2
  277.6 26.2 %convolution_reduce_fusion.2 = f32[384]{0:T(512)S(1)} fusion(f32[16384,1]{0,1:T(1,128)S(1)} %bitcast.20, f32[384,16384]{1,0:T(8,128)} %get-tuple-element.5, f32[384]{0:T(512)S(1)} %pmax.7), kind=kOutput, calls=%fused_computation.11 | convolution fusion | flops 81788928 | bytes 25234432 | tf_op jit(solution)/shard_map/dot_general | solution.py:23
  303.8 5.8 psum.51
  309.7 18.6 %fusion.9 = f32[1,16384]{1,0:T(1,128)} fusion(f32[384,1]{0,1:T(1,128)S(1)} %reshape.14, f32[384,16384]{1,0:T(8,128)} %get-tuple-element.5, f32[384]{0:T(512)S(1)} %pmax.7), kind=kOutput, calls=%fused_computation.20 | convolution fusion | flops 81788928 | bytes 25234432 | tf_op jit(solution)/shard_map/dot_general | solution.py:28
  328.4 68.8 %all-reduce.8.cloned.1.call-done = f32[16384]{0:T(1024)} async-done(((f32[16384]{0:T(1024)}), f32[16384]{0:T(1024)}) %all-reduce.8.cloned.1.call-update) | async-done | bytes 65552 | tf_op jit(solution)/shard_map/psum | solution.py:29
  398.0 26.2 %convolution_reduce_fusion.1 = f32[384]{0:T(512)S(1)} fusion(f32[16384,1]{0,1:T(1,128)S(1)} %bitcast.21, f32[384,16384]{1,0:T(8,128)} %get-tuple-element.5, f32[384]{0:T(512)S(1)} %pmax.7), kind=kOutput, calls=%fused_computation.10 | convolution fusion | flops 81788928 | bytes 25234432 | tf_op jit(solution)/shard_map/dot_general | solution.py:23
  424.2 5.9 psum.53
  430.1 18.6 %fusion.8 = f32[1,16384]{1,0:T(1,128)} fusion(f32[384,1]{0,1:T(1,128)S(1)} %reshape.18, f32[384,16384]{1,0:T(8,128)} %get-tuple-element.5, f32[384]{0:T(512)S(1)} %pmax.7), kind=kOutput, calls=%fused_computation.19 | convolution fusion | flops 81788928 | bytes 25234432 | tf_op jit(solution)/shard_map/dot_general | solution.py:28
  448.8 68.8 %all-reduce.10.cloned.1.call-done = f32[16384]{0:T(1024)} async-done(((f32[16384]{0:T(1024)}), f32[16384]{0:T(1024)}) %all-reduce.10.cloned.1.call-update) | async-done | bytes 65552 | tf_op jit(solution)/shard_map/psum | solution.py:29
  518.4 26.2 %convolution_reduce_fusion = f32[384]{0:T(512)S(1)} fusion(f32[16384,1]{0,1:T(1,128)S(1)} %bitcast.16, f32[384,16384]{1,0:T(8,128)} %get-tuple-element.5, f32[384]{0:T(512)S(1)} %pmax.7), kind=kOutput, calls=%fused_computation.9 | convolution fusion | flops 81788928 | bytes 25234432 | tf_op jit(solution)/shard_map/dot_general | solution.py:23
  544.6 5.7 psum.55
  550.3 11.9 %fusion.1 = f32[16384]{0:T(1024)} fusion(f32[16384]{0:T(1024)S(1)} %broadcast_divide_fusion, f32[384]{0:T(512)S(1)} %div.39, f32[384,16384]{1,0:T(8,128)} %get-tuple-element.5, f32[384]{0:T(512)S(1)} %pmax.7), kind=kLoop, calls=%fused_computation.4 | loop fusion | flops 25149440 | bytes 25299968 | tf_op jit(solution)/shard_map/reduce_sum | solution.py:32
  562.6 14.9 %fusion.2 = f32[16384,256]{1,0:T(8,128)} fusion(bf16[384,256]{1,0:T(8,128)(2,1)S(1)} %copy-done, f32[16384]{0:T(1024)S(1)} %broadcast_divide_fusion, f32[384]{0:T(512)S(1)} %div.39, f32[384,16384]{1,0:T(8,128)} %get-tuple-element.5, f32[384]{0:T(512)S(1)} %pmax.7), kind=kOutput, calls=%fused_computation.5 | convolution fusion | flops 3246391296 | bytes 42208256 | tf_op jit(solution)/shard_map/nk,nd->kd/dot_general | solution.py:33
  578.8 52.3 %all-reduce.12.cloned.1.call-done = f32[16384]{0:T(1024)} async-done(((f32[16384]{0:T(1024)}), f32[16384]{0:T(1024)}) %all-reduce.12.cloned.1.call-update) | async-done | bytes 65552
  631.1 1.3 broadcast_multiply_fusion
  632.4 284.8 %reduce-scatter.2.cloned.1.call-done = f32[2048,256]{1,0:T(8,128)} async-done(((f32[16384,256]{1,0:T(8,128)}), f32[2048,256]{1,0:T(8,128)}) %reduce-scatter.2.cloned.1.call-update) | async-done | bytes 2097168 | tf_op jit(solution)/shard_map/reduce_scatter | solution.py:40
  917.2 3.3 subtract_multiply_fusion
  (30 shorter events, 3.6 us)
Async XLA Ops:
  7.2 130.6 %copy-start = (bf16[384,256]{1,0:T(8,128)(2,1)S(1)}, bf16[384,256]{1,0:T(8,128)(2,1)}, u32[]{:S(2)}) copy-start(bf16[384,256]{1,0:T(8,128)(2,1)} %param.3) | copy-start | bytes 589828
  7.2 130.6 %all-gather.2.cloned.1.call-start = ((), (), s32[]{:S(2)}) async-start(), calls=%async_computation.1 | async-start | bytes 9437184 | tf_op jit(solution)/shard_map/all_gather | solution.py:16
  7.9 183.9 %copy-start.2 = (f32[384]{0:T(512)S(1)}, f32[384]{0:T(512)}, u32[]{:S(2)}) copy-start(f32[384]{0:T(512)} %param.5) | copy-start | bytes 4612
  7.9 268.8 %all-reduce.6.cloned.1.call-start = ((), (), s32[]{:S(2)}) async-start(), calls=%async_computation.2 | async-start | bytes 131072 | tf_op jit(solution)/shard_map/psum | solution.py:29
  210.5 186.6 %all-reduce.8.cloned.1.call-start = ((), (), s32[]{:S(2)}) async-start(), calls=%async_computation.3 | async-start | bytes 131072 | tf_op jit(solution)/shard_map/psum | solution.py:29
  328.3 189.3 %all-reduce.10.cloned.1.call-start = ((), (), s32[]{:S(2)}) async-start(), calls=%async_computation.4 | async-start | bytes 131072 | tf_op jit(solution)/shard_map/psum | solution.py:29
  448.7 182.4 %all-reduce.12.cloned.1.call-start = ((), (), s32[]{:S(2)}) async-start(), calls=%async_computation.6 | async-start | bytes 131072
  562.3 15.3 %copy-start.3 = (u32[32]{0:T(128)S(1)}, u32[32]{0:T(128)}, u32[]{:S(2)}) copy-start(u32[32]{0:T(128)} %constant.17) | copy-start | bytes 388
  562.3 354.9 %copy-start.1 = (bf16[2048,256]{1,0:T(8,128)(2,1)S(1)}, bf16[2048,256]{1,0:T(8,128)(2,1)}, u32[]{:S(2)}) copy-start(bf16[2048,256]{1,0:T(8,128)(2,1)} %param.4) | copy-start | bytes 3145732
  562.3 354.9 %reduce-scatter.2.cloned.1.call-start = ((), (), s32[]{:S(2)}) async-start(), calls=%async_computation.5 | async-start | bytes 18874368 | tf_op jit(solution)/shard_map/reduce_scatter | solution.py:40
Sparse Core Ops, SparseCore 0:
  10.1 127.6 all-gather.1
  210.6 66.0 all-reduce.5
  328.4 68.6 all-reduce.7
  448.9 68.6 all-reduce.9
  562.4 68.6 all-reduce.11
  634.7 282.4 reduce-scatter.1
where the time goes:
time: 935 us; the launch traced here: 928 us
  waiting for transfers between devices  671 us (72%)
  matrix products  191 us (20%)
  blocking collectives  30.1 us (3%)
  other arithmetic  19.1 us (2%)
  between operations  15.1 us (2%)
    reduce_scatter x1, waiting for transfers between devices, local(): lax.psum_scatter(partial_aggregates, 'rows', scatter_dimension=0, tiled=T...  285 us
    psum x3, waiting for transfers between devices, local(): col_scale = balance / lax.psum(partial_cols, 'rows')  204 us
    all_gather x1, waiting for transfers between devices, local(): lax.all_gather(codebook, 'rows', axis=0, tiled=True)  130 us
    dot_general x4, matrix products, marginal_per_sample(): jnp.dot(power_term, col_scale, precision=lax.Precision.HIGHEST)  105 us
    dot_general x3, matrix products, local(): jnp.dot(row_scale, power_term, precision=lax.Precision.HIGHEST)  55.9 us
    unnamed x7, waiting for transfers between devices  53.1 us
    psum x4, blocking collectives, marginal_per_sample(): lax.psum(jnp.dot(power_term, col_scale, precision=lax.Precision.HIGHEST),...  24 us
  transfers between devices with their start and end apart: 6, of which 6 were waited for; matrix products, arithmetic and copies ran while one was open for 2% of the time, Pallas kernels for 0%

commit v1 on v0

--- a/solution.py
+++ b/solution.py
@@ -8,13 +8,37 @@
 
 
 def local(embedding_vectors, codebook, weights):
+
+    def arrays_state(piece_in, dim_k, xin, which_dim):
+        t1 = lax.psum(1, axis_name="rows")
+        view_out = lax.axis_index("rows")
+        lower, local_out, built = (t1, view_out, piece_in.shape[dim_k])
+        buffers = []
+        p = 0
+        while p < lower:
+            moved = (
+                lax.ppermute(
+                    piece_in, axis_name="rows", perm=[(h, (h + 1) % lower) for h in range(lower)]
+                )
+                if p + 1 < lower
+                else piece_in
+            )
+            b_now = xin(piece_in, (local_out - p) % lower * built)
+            buffers.append(b_now)
+            piece_in = moved
+            p = p + 1
+        f_next = jnp.concatenate(buffers[::-1], which_dim)
+        return jnp.roll(f_next, (local_out + 1) * buffers[0].shape[which_dim], which_dim)
+
     code_devices = lax.axis_size("code")
     balance = embedding_vectors.shape[0] / (code_devices * codebook.shape[0])
-    similarity_table = sharpness_factor * jnp.einsum(
-        "nd,kd->nk",
-        embedding_vectors,
-        lax.all_gather(codebook, "rows", axis=0, tiled=True),
-        preferred_element_type=jnp.float32,
+    similarity_table = sharpness_factor * arrays_state(
+        codebook,
+        0,
+        lambda part, at: jnp.einsum(
+            "nd,kd->nk", embedding_vectors, part, preferred_element_type=jnp.float32
+        ),
+        1,
     )
     row_peak = lax.pmax(jnp.max(similarity_table, axis=1), "code")
     power_term = jnp.exp(similarity_table - row_peak[:, None])

time: 935 us -> 1020 us (1.091)
  waiting for transfers between devices: 671 us -> 715 us
  local copies, waits for them, and re-layouts: 0.63 us -> 18 us
  matrix products: 191 us -> 204 us
    ppermute x0 -> x7, waiting for transfers between devices: none -> 175 us  [arrays_state(): lax.ppermute(piece_in, axis_name='rows', perm=[(h, (h + 1) % lower) for h...]
    all_gather x1 -> x0, waiting for transfers between devices: 130 us -> none  [local(): lax.all_gather(codebook, 'rows', axis=0, tiled=True)]
    unnamed x9 -> x24, local copies, waits for them, and re-layouts: 0.61 us -> 16.1 us
    dot_general x1 -> x8, matrix products: 15.2 us -> 22.6 us  [local(): jnp.einsum('nd,kd->nk', embedding_vectors, part, preferred_element_type=j...]
    unnamed x7 -> x6, waiting for transfers between devices: 53.1 us -> 52.2 us
  transfers between devices with their start and end apart: 6 -> 12, of which waited for: 6 -> 12; matrix products, arithmetic and copies ran while one was open for 2% -> 2% of each run, Pallas kernels for 0% -> 0%
where the time goes in v1:
time: 1020 us; the launch traced here: 1010 us
  waiting for transfers between devices  715 us (70%)
  matrix products  204 us (20%)
  other arithmetic  28.8 us (3%)
  blocking collectives  28.7 us (3%)
  local copies, waits for them, and re-layouts  18 us (2%)
  between operations  14.7 us (1%)
    reduce_scatter x1, waiting for transfers between devices, local(): lax.psum_scatter(partial_aggregates, 'rows', scatter_dimension=0, tiled=T...  285 us
    psum x3, waiting for transfers between devices, local(): col_scale = balance / lax.psum(partial_cols, 'rows')  202 us
    ppermute x7, waiting for transfers between devices, arrays_state(): lax.ppermute(piece_in, axis_name='rows', perm=[(h, (h + 1) % lower) for h...  175 us
    dot_general x4, matrix products, marginal_per_sample(): jnp.dot(power_term, col_scale, precision=lax.Precision.HIGHEST)  108 us
    dot_general x3, matrix products, local(): jnp.dot(row_scale, power_term, precision=lax.Precision.HIGHEST)  58 us
    unnamed x6, waiting for transfers between devices  52.2 us
    psum x4, blocking collectives, marginal_per_sample(): lax.psum(jnp.dot(power_term, col_scale, precision=lax.Precision.HIGHEST),...  22.8 us
    dot_general x8, matrix products, local(): jnp.einsum('nd,kd->nk', embedding_vectors, part, preferred_element_type=j...  22.6 us
  transfers between devices with their start and end apart: 12, of which 12 were waited for; matrix products, arithmetic and copies ran while one was open for 2% of the time, Pallas kernels for 0%

profile of v1, /device:TPU:0, one launch (start us, length us, event | category | flops | bytes accessed | tf_op | source)
XLA Modules:
  0.0 1012.8 jit_solution(14940308830050471974)
XLA Ops:
  10.2 26.4 %collective-permute-done = bf16[2048,256]{1,0:T(8,128)(2,1)S(1)} collective-permute-done((bf16[2048,256]{1,0:T(8,128)(2,1)}, bf16[2048,256]{1,0:T(8,128)(2,1)S(1)}, u32[]{:S(2)}, u32[]{:S(2)}) %collective-permute-start) | collective-permute-done | bytes 1048608 | tf_op jit(solution)/shard_map/ppermute | solution.py:20
  36.7 27.0 %collective-permute-done.1 = bf16[2048,256]{1,0:T(8,128)(2,1)S(1)} collective-permute-done((bf16[2048,256]{1,0:T(8,128)(2,1)S(1)}, bf16[2048,256]{1,0:T(8,128)(2,1)S(1)}, u32[]{:S(2)}, u32[]{:S(2)}) %collective-permute-start.1) | collective-permute-done | bytes 1048608 | tf_op jit(solution)/shard_map/ppermute | solution.py:20
  63.7 26.1 %collective-permute-done.2 = bf16[2048,256]{1,0:T(8,128)(2,1)S(1)} collective-permute-done((bf16[2048,256]{1,0:T(8,128)(2,1)S(1)}, bf16[2048,256]{1,0:T(8,128)(2,1)S(1)}, u32[]{:S(2)}, u32[]{:S(2)}) %collective-permute-start.2) | collective-permute-done | bytes 1048608 | tf_op jit(solution)/shard_map/ppermute | solution.py:20
  90.8 25.2 %collective-permute-done.3 = bf16[2048,256]{1,0:T(8,128)(2,1)S(1)} collective-permute-done((bf16[2048,256]{1,0:T(8,128)(2,1)S(1)}, bf16[2048,256]{1,0:T(8,128)(2,1)S(1)}, u32[]{:S(2)}, u32[]{:S(2)}) %collective-permute-start.3) | collective-permute-done | bytes 1048608 | tf_op jit(solution)/shard_map/ppermute | solution.py:20
  117.0 24.3 %collective-permute-done.4 = bf16[2048,256]{1,0:T(8,128)(2,1)S(1)} collective-permute-done((bf16[2048,256]{1,0:T(8,128)(2,1)S(1)}, bf16[2048,256]{1,0:T(8,128)(2,1)S(1)}, u32[]{:S(2)}, u32[]{:S(2)}) %collective-permute-start.4) | collective-permute-done | bytes 1048608 | tf_op jit(solution)/shard_map/ppermute | solution.py:20
  142.2 23.5 %collective-permute-done.5 = bf16[2048,256]{1,0:T(8,128)(2,1)} collective-permute-done((bf16[2048,256]{1,0:T(8,128)(2,1)S(1)}, bf16[2048,256]{1,0:T(8,128)(2,1)}, u32[]{:S(2)}, u32[]{:S(2)}) %collective-permute-start.5) | collective-permute-done | bytes 1048608 | tf_op jit(solution)/shard_map/ppermute | solution.py:20
  165.7 22.7 %collective-permute-done.6 = bf16[2048,256]{1,0:T(8,128)(2,1)} collective-permute-done((bf16[2048,256]{1,0:T(8,128)(2,1)}, bf16[2048,256]{1,0:T(8,128)(2,1)}, u32[]{:S(2)}, u32[]{:S(2)}) %collective-permute-start.6) | collective-permute-done | bytes 1048608 | tf_op jit(solution)/shard_map/ppermute | solution.py:20
  225.4 9.4 fusion.2
  234.8 5.9 pmax.7
  240.8 26.9 %convolution_reduce_fusion.3 = f32[384]{0:T(512)S(1)} fusion(f32[384,32768]{1,0:T(8,128)} %constant_dynamic-update-slice_fusion, s32[]{:T(128)S(6)} %select_n.14, f32[384]{0:T(512)S(1)} %pmax.7), kind=kOutput, calls=%fused_computation.13 | convolution fusion | flops 88080384 | bytes 25168900 | tf_op jit(solution)/shard_map/dot_general | solution.py:47
  267.7 5.8 psum.49
  273.5 19.4 %fusion.11 = f32[1,16384]{1,0:T(1,128)} fusion(f32[384,1]{0,1:T(1,128)S(1)} %reshape.10, f32[384,32768]{1,0:T(8,128)} %constant_dynamic-update-slice_fusion, s32[]{:T(128)S(6)} %select_n.14, f32[384]{0:T(512)S(1)} %pmax.7), kind=kOutput, calls=%fused_computation.38 | convolution fusion | flops 88080384 | bytes 25234436 | tf_op jit(solution)/shard_map/dot_general | solution.py:52
  293.1 65.4 %all-reduce.6.cloned.1.call-done = f32[16384]{0:T(1024)} async-done(((f32[16384]{0:T(1024)}), f32[16384]{0:T(1024)}) %all-reduce.6.cloned.1.call-update) | async-done | bytes 65552 | tf_op jit(solution)/shard_map/psum | solution.py:53
  359.4 27.0 %convolution_reduce_fusion.2 = f32[384]{0:T(512)S(1)} fusion(f32[16384,1]{0,1:T(1,128)S(1)} %bitcast.34, f32[384,32768]{1,0:T(8,128)} %constant_dynamic-update-slice_fusion, s32[]{:T(128)S(6)} %select_n.14, f32[384]{0:T(512)S(1)} %pmax.7), kind=kOutput, calls=%fused_computation.12 | convolution fusion | flops 88080384 | bytes 25234436 | tf_op jit(solution)/shard_map/dot_general | solution.py:47
  392.1 19.3 %fusion.10 = f32[1,16384]{1,0:T(1,128)} fusion(f32[384,1]{0,1:T(1,128)S(1)} %reshape.14, f32[384,32768]{1,0:T(8,128)} %constant_dynamic-update-slice_fusion, s32[]{:T(128)S(6)} %select_n.14, f32[384]{0:T(512)S(1)} %pmax.7), kind=kOutput, calls=%fused_computation.37 | convolution fusion | flops 88080384 | bytes 25234436 | tf_op jit(solution)/shard_map/dot_general | solution.py:52
  411.9 68.4 %all-reduce.8.cloned.1.call-done = f32[16384]{0:T(1024)} async-done(((f32[16384]{0:T(1024)}), f32[16384]{0:T(1024)}) %all-reduce.8.cloned.1.call-update) | async-done | bytes 65552 | tf_op jit(solution)/shard_map/psum | solution.py:53
  481.1 27.0 %convolution_reduce_fusion.1 = f32[384]{0:T(512)S(1)} fusion(f32[16384,1]{0,1:T(1,128)S(1)} %bitcast.35, f32[384,32768]{1,0:T(8,128)} %constant_dynamic-update-slice_fusion, s32[]{:T(128)S(6)} %select_n.14, f32[384]{0:T(512)S(1)} %pmax.7), kind=kOutput, calls=%fused_computation.11 | convolution fusion | flops 88080384 | bytes 25234436 | tf_op jit(solution)/shard_map/dot_general | solution.py:47
  513.8 19.3 %fusion.9 = f32[1,16384]{1,0:T(1,128)} fusion(f32[384,1]{0,1:T(1,128)S(1)} %reshape.18, f32[384,32768]{1,0:T(8,128)} %constant_dynamic-update-slice_fusion, s32[]{:T(128)S(6)} %select_n.14, f32[384]{0:T(512)S(1)} %pmax.7), kind=kOutput, calls=%fused_computation.36 | convolution fusion | flops 88080384 | bytes 25234436 | tf_op jit(solution)/shard_map/dot_general | solution.py:52
  533.4 68.6 %all-reduce.10.cloned.1.call-done = f32[16384]{0:T(1024)} async-done(((f32[16384]{0:T(1024)}), f32[16384]{0:T(1024)}) %all-reduce.10.cloned.1.call-update) | async-done | bytes 65552 | tf_op jit(solution)/shard_map/psum | solution.py:53
  602.9 27.0 %convolution_reduce_fusion = f32[384]{0:T(512)S(1)} fusion(f32[16384,1]{0,1:T(1,128)S(1)} %bitcast.30, f32[384,32768]{1,0:T(8,128)} %constant_dynamic-update-slice_fusion, s32[]{:T(128)S(6)} %select_n.14, f32[384]{0:T(512)S(1)} %pmax.7), kind=kOutput, calls=%fused_computation.10 | convolution fusion | flops 88080384 | bytes 25234436 | tf_op jit(solution)/shard_map/dot_general | solution.py:47
  635.5 12.3 %fusion.1 = f32[16384]{0:T(1024)} fusion(f32[16384]{0:T(1024)S(1)} %broadcast_divide_fusion, f32[384]{0:T(512)S(1)} %div.39, f32[384]{0:T(512)S(1)} %pmax.7, f32[384,32768]{1,0:T(8,128)} %constant_dynamic-update-slice_fusion, s32[]{:T(128)S(6)} %select_n.14), kind=kLoop, calls=%fused_computation.4 | loop fusion | flops 31440896 | bytes 25299972 | tf_op jit(solution)/shard_map/reduce_sum | solution.py:56
  647.9 15.4 %fusion.3 = f32[16384,256]{1,0:T(8,128)} fusion(bf16[384,256]{1,0:T(8,128)(2,1)S(1)} %copy-done, f32[16384]{0:T(1024)S(1)} %broadcast_divide_fusion, f32[384]{0:T(512)S(1)} %div.39, f32[384,32768]{1,0:T(8,128)} %constant_dynamic-update-slice_fusion, s32[]{:T(128)S(6)} %select_n.14, f32[384]{0:T(512)S(1)} %pmax.7), kind=kOutput, calls=%fused_computation.6 | convolution fusion | flops 3252682752 | bytes 42208260 | tf_op jit(solution)/shard_map/nk,nd->kd/dot_general | solution.py:57
  664.6 52.1 %all-reduce.12.cloned.1.call-done = f32[16384]{0:T(1024)} async-done(((f32[16384]{0:T(1024)}), f32[16384]{0:T(1024)}) %all-reduce.12.cloned.1.call-update) | async-done | bytes 65552
  718.0 284.9 %reduce-scatter.2.cloned.1.call-done = f32[2048,256]{1,0:T(8,128)} async-done(((f32[16384,256]{1,0:T(8,128)}), f32[2048,256]{1,0:T(8,128)}) %reduce-scatter.2.cloned.1.call-update) | async-done | bytes 2097168 | tf_op jit(solution)/shard_map/reduce_scatter | solution.py:64
  (65 shorter events, 68.8 us)
Async XLA Ops:
  7.2 181.3 %copy-start = (bf16[384,256]{1,0:T(8,128)(2,1)S(1)}, bf16[384,256]{1,0:T(8,128)(2,1)}, u32[]{:S(2)}) copy-start(bf16[384,256]{1,0:T(8,128)(2,1)} %param.3) | copy-start | bytes 589828
  7.2 351.4 %all-reduce.6.cloned.1.call-start = ((), (), s32[]{:S(2)}) async-start(), calls=%async_computation.1 | async-start | bytes 131072 | tf_op jit(solution)/shard_map/psum | solution.py:53
  7.2 29.4 %collective-permute-start = (bf16[2048,256]{1,0:T(8,128)(2,1)}, bf16[2048,256]{1,0:T(8,128)(2,1)S(1)}, u32[]{:S(2)}, u32[]{:S(2)}) collective-permute-start(bf16[2048,256]{1,0:T(8,128)(2,1)} %param.4), channel_id=1, source_target_pairs={{0,4},{4,8},{8,12},{12,16},{16,20},{20,24},{24,28},{28,0},{1,5},{5... | collective-permute-start | bytes 3145736 | tf_op jit(solution)/shard_map/ppermute | solution.py:20
  36.7 27.0 %collective-permute-start.1 = (bf16[2048,256]{1,0:T(8,128)(2,1)S(1)}, bf16[2048,256]{1,0:T(8,128)(2,1)S(1)}, u32[]{:S(2)}, u32[]{:S(2)}) collective-permute-start(bf16[2048,256]{1,0:T(8,128)(2,1)S(1)} %collective-permute-done), channel_id=1, source_target_pairs={{0,4},{4,8},{8,12},{12,16},{16,20},{20,24},{24,28},{28,0},{1,5},{5... | collective-permute-start | bytes 3145736 | tf_op jit(solution)/shard_map/ppermute | solution.py:20
  63.7 26.1 %collective-permute-start.2 = (bf16[2048,256]{1,0:T(8,128)(2,1)S(1)}, bf16[2048,256]{1,0:T(8,128)(2,1)S(1)}, u32[]{:S(2)}, u32[]{:S(2)}) collective-permute-start(bf16[2048,256]{1,0:T(8,128)(2,1)S(1)} %collective-permute-done.1), channel_id=1, source_target_pairs={{0,4},{4,8},{8,12},{12,16},{16,20},{20,24},{24,28},{28,0},{1,5},{5... | collective-permute-start | bytes 3145736 | tf_op jit(solution)/shard_map/ppermute | solution.py:20
  89.8 1.0 copy-start.2
  90.8 25.2 %collective-permute-start.3 = (bf16[2048,256]{1,0:T(8,128)(2,1)S(1)}, bf16[2048,256]{1,0:T(8,128)(2,1)S(1)}, u32[]{:S(2)}, u32[]{:S(2)}) collective-permute-start(bf16[2048,256]{1,0:T(8,128)(2,1)S(1)} %collective-permute-done.2), channel_id=1, source_target_pairs={{0,4},{4,8},{8,12},{12,16},{16,20},{20,24},{24,28},{28,0},{1,5},{5... | collective-permute-start | bytes 3145736 | tf_op jit(solution)/shard_map/ppermute | solution.py:20
  116.0 1.0 copy-start.4
  117.0 24.3 %collective-permute-start.4 = (bf16[2048,256]{1,0:T(8,128)(2,1)S(1)}, bf16[2048,256]{1,0:T(8,128)(2,1)S(1)}, u32[]{:S(2)}, u32[]{:S(2)}) collective-permute-start(bf16[2048,256]{1,0:T(8,128)(2,1)S(1)} %collective-permute-done.3), channel_id=1, source_target_pairs={{0,4},{4,8},{8,12},{12,16},{16,20},{20,24},{24,28},{28,0},{1,5},{5... | collective-permute-start | bytes 3145736 | tf_op jit(solution)/shard_map/ppermute | solution.py:20
  141.3 1.0 copy-start.5
  142.2 23.5 %collective-permute-start.5 = (bf16[2048,256]{1,0:T(8,128)(2,1)S(1)}, bf16[2048,256]{1,0:T(8,128)(2,1)}, u32[]{:S(2)}, u32[]{:S(2)}) collective-permute-start(bf16[2048,256]{1,0:T(8,128)(2,1)S(1)} %collective-permute-done.4), channel_id=1, source_target_pairs={{0,4},{4,8},{8,12},{12,16},{16,20},{20,24},{24,28},{28,0},{1,5},{5... | collective-permute-start | bytes 3145736 | tf_op jit(solution)/shard_map/ppermute | solution.py:20
  165.7 22.8 %collective-permute-start.6 = (bf16[2048,256]{1,0:T(8,128)(2,1)}, bf16[2048,256]{1,0:T(8,128)(2,1)}, u32[]{:S(2)}, u32[]{:S(2)}) collective-permute-start(bf16[2048,256]{1,0:T(8,128)(2,1)} %collective-permute-done.5), channel_id=1, source_target_pairs={{0,4},{4,8},{8,12},{12,16},{16,20},{20,24},{24,28},{28,0},{1,5},{5... | collective-permute-start | bytes 3145736 | tf_op jit(solution)/shard_map/ppermute | solution.py:20
  165.7 36.5 %copy-start.3 = (bf16[2048,256]{1,0:T(8,128)(2,1)S(1)}, bf16[2048,256]{1,0:T(8,128)(2,1)}, u32[]{:S(2)}) copy-start(bf16[2048,256]{1,0:T(8,128)(2,1)} %copy-done.2) | copy-start | bytes 3145732
  165.7 43.1 %copy-start.1 = (bf16[2048,256]{1,0:T(8,128)(2,1)S(1)}, bf16[2048,256]{1,0:T(8,128)(2,1)}, u32[]{:S(2)}) copy-start(bf16[2048,256]{1,0:T(8,128)(2,1)} %param.4) | copy-start | bytes 3145732
  225.4 48.1 %copy-start.6 = (f32[384]{0:T(512)S(1)}, f32[384]{0:T(512)}, u32[]{:S(2)}) copy-start(f32[384]{0:T(512)} %param.5) | copy-start | bytes 4612
  292.9 187.4 %all-reduce.8.cloned.1.call-start = ((), (), s32[]{:S(2)}) async-start(), calls=%async_computation.2 | async-start | bytes 131072 | tf_op jit(solution)/shard_map/psum | solution.py:53
  411.4 190.6 %all-reduce.10.cloned.1.call-start = ((), (), s32[]{:S(2)}) async-start(), calls=%async_computation.3 | async-start | bytes 131072 | tf_op jit(solution)/shard_map/psum | solution.py:53
  533.2 183.5 %all-reduce.12.cloned.1.call-start = ((), (), s32[]{:S(2)}) async-start(), calls=%async_computation.5 | async-start | bytes 131072
  647.9 15.4 %copy-start.7 = (u32[32]{0:T(128)S(1)}, u32[32]{0:T(128)}, u32[]{:S(2)}) copy-start(u32[32]{0:T(128)} %constant.49) | copy-start | bytes 388
  647.9 355.0 %reduce-scatter.2.cloned.1.call-start = ((), (), s32[]{:S(2)}) async-start(), calls=%async_computation.4 | async-start | bytes 18874368 | tf_op jit(solution)/shard_map/reduce_scatter | solution.py:64
Sparse Core Ops, SparseCore 0:
  293.0 65.5 all-reduce.5
  411.6 68.6 all-reduce.7
  533.3 68.6 all-reduce.9
  648.0 68.6 all-reduce.11
  720.3 282.4 reduce-scatter.1
